TPU v7x, 32 devices: a whole 2x2x4 slice. The times are simulated.
32 devices in a mesh: case: 2 (over x), ax: 16 (over z, y, core).
Axes of the slice: x: 2, y: 2, z: 4, core: 2. Of those that a mesh axis runs over, the one named last changes fastest.
Arguments:
- populations: float32 [19, 32, 128, 128], P(None, 'ax', 'case'), parts along dimension 2, may hold values from 0 to 1, as said below
- solid_mask: int32 [32, 128, 128], P('ax', 'case'), parts along dimension 1, may hold values from 0 to 1, as said below
- link_flags: int32 [2, 32, 128, 128], P(None, 'ax', 'case'), parts along dimension 2, may hold values from 0 to 511, as said below
- inlet_cells: int32 [1024], P('case'), parts along dimension 0, may hold values from 0 to 8191, as said below
- pod_basis: float32 [512, 3, 512], P(None, None, 'ax'), may hold values from -0.15625 to 0.15625
- mri_frames: float32 [24, 6, 512], P(None, 'case', 'ax'), parts along dimension 1
- frame_index: int32 [1], replicated, may hold values from 0 to 23
Outputs:
- advanced_populations: float32 [19, 32, 128, 128], P(None, 'ax', 'case'), parts along dimension 2
- inflow: float32 [2, 6, 512], P(None, 'case', 'ax'), parts along dimension 1
There are 2 independent parts, one for each index of `case`. A program takes and returns all parts, laid end to end along the dimension named above; an argument that names none is the same for every part. Nothing has to cross between parts.
Inputs may be any that keep to these rules, and one draw needn't show every extreme that they name: `solid_mask`: 1 marks a wall cell, 0 a fluid cell; the two outermost rows and columns of every cross-section are wall cells. `link_flags`: at a fluid cell, bit (i - 1) mod 9 of word (i - 1) div 9 is set exactly when the cell at minus c_i is a wall cell, the grid being continued past its first and last plane by repeating those planes; zero at wall cells. `inlet_cells`: distinct cells of the first plane, all of them fluid cells. `populations`: every entry is positive.
All inputs are finite; a program needn't handle non-finite values.
Results may differ from a plain program's by a relative error of at most 0.00011.
Values sent between devices are 32-bit elements; how exact they have to be, the bound alone decides.
A program may use at most 64 MiB of HBM per device.

v0:
```python
import math
import jax
import jax.numpy as jnp
from jax import lax
from jax.sharding import PartitionSpec as P

STEPS = 2
lattice_c = (
    (0, 0, 0),
    (1, 0, 0),
    (-1, 0, 0),
    (0, 1, 0),
    (0, -1, 0),
    (0, 0, 1),
    (0, 0, -1),
    (1, 1, 0),
    (-1, -1, 0),
    (1, -1, 0),
    (-1, 1, 0),
    (1, 0, 1),
    (-1, 0, -1),
    (1, 0, -1),
    (-1, 0, 1),
    (0, 1, 1),
    (0, -1, -1),
    (0, 1, -1),
    (0, -1, 1),
)
lattice_w = (1.0 / 3.0,) + (1.0 / 18.0,) * 6 + (1.0 / 36.0,) * 12
opposite_of = (0, 2, 1, 4, 3, 6, 5, 8, 7, 10, 9, 12, 11, 14, 13, 16, 15, 18, 17)
pair_list = ((0, 0), (1, 1), (2, 2), (0, 1), (0, 2), (1, 2))
relax_base = 0.52
smagorinsky_sq = 0.04
inflow_scale = 0.05


def extended(array, sides, width):
    for axis, dim in sides:
        count, length = (lax.axis_size(axis), array.shape[dim])
        up = [(i, (i + 1) % count) for i in range(count - 1)]
        down = [(j, i) for i, j in up]
        last = lax.slice_in_dim(array, length - width, length, axis=dim)
        leading = lax.slice_in_dim(array, 0, width, axis=dim)
        before = lax.ppermute(last, axis, up)
        after = lax.ppermute(leading, axis, down)
        array = jnp.concatenate([before, array, after], axis=dim)
    return array


def moment_rows():
    listed = [[1.0] * 19]
    for axis_a in range(3):
        listed.append([float(vector[axis_a]) for vector in lattice_c])
    for pair_a, pair_b in pair_list:
        listed.append([float(vector[pair_a] * vector[pair_b]) for vector in lattice_c])
    return jnp.asarray(listed, dtype=jnp.float32)


def equilibrium(density, velocity):
    lattice = jnp.asarray(
        [[float(entry) for entry in vector] for vector in lattice_c], dtype=jnp.float32
    )
    weights = jnp.asarray(list(lattice_w), dtype=jnp.float32).reshape((19,) + (1,) * density.ndim)
    projected = jnp.einsum("iq,q...->i...", lattice, velocity, precision=lax.Precision.HIGHEST)
    speed_sq = jnp.sum(velocity * velocity, axis=0)
    return (
        weights
        * density[None]
        * (1.0 + 3.0 * projected + 4.5 * projected * projected - 1.5 * speed_sq[None])
    )


def collide(populations, solid_mask):
    moments = jnp.einsum(
        "mi,i...->m...", moment_rows(), populations, precision=lax.Precision.HIGHEST
    )
    density = moments[0]
    velocity = moments[1:4] / density[None]
    nonequil = populations - equilibrium(density, velocity)
    stress = jnp.einsum(
        "mi,i...->m...", moment_rows()[4:], nonequil, precision=lax.Precision.HIGHEST
    )
    magnitude = stress[0] * stress[0] + stress[1] * stress[1] + stress[2] * stress[2]
    magnitude = magnitude + 2.0 * (
        stress[3] * stress[3] + stress[4] * stress[4] + stress[5] * stress[5]
    )
    relax_time = 0.5 * (
        relax_base
        + jnp.sqrt(
            relax_base * relax_base
            + 18.0 * math.sqrt(2.0) * smagorinsky_sq * jnp.sqrt(magnitude) / density
        )
    )
    relaxed = populations - nonequil / relax_time[None]
    return jnp.where(solid_mask[None] == 1, populations, relaxed)


def stream(relaxed, ghost_low, ghost_high, link_flags, solid_mask):
    padded = jnp.concatenate([ghost_low[:, None], relaxed, ghost_high[:, None]], axis=1)
    planes_here = relaxed.shape[1]
    read = []
    for direction in range(19):
        step_x, step_y, step_z = lattice_c[direction]
        source = padded[direction, 1 - step_z : 1 - step_z + planes_here]
        source = jnp.roll(source, (step_y, step_x), axis=(1, 2))
        if direction > 0:
            word = link_flags[(direction - 1) // 9]
            linked = jnp.bitwise_and(jnp.right_shift(word, (direction - 1) % 9), 1)
            source = jnp.where(linked == 1, relaxed[opposite_of[direction]], source)
        read.append(jnp.where(solid_mask == 1, relaxed[direction], source))
    return jnp.stack(read)


def inlet_plane(speeds, inlet_cells, height, plane_width):
    inlet_speed = jnp.zeros((3, height * plane_width), jnp.float32).at[:, inlet_cells].set(speeds)
    inlet_speed = inlet_speed.reshape(3, height, plane_width)
    return equilibrium(jnp.ones((height, plane_width), jnp.float32), inlet_speed)


def neighbour_planes(relaxed):
    padded = extended(relaxed, (("ax", 1),), 1)
    ghost_low = padded[:, 0]
    ghost_high = padded[:, -1]
    return (ghost_low, ghost_high)


def body(populations, solid_mask, link_flags, inlet_cells, pod_basis, mri_frames, frame_index):
    frames_total = mri_frames.shape[0]
    frame_slot = lax.broadcasted_iota(jnp.int32, (STEPS, frames_total), 1)
    segment_slot = lax.broadcasted_iota(jnp.int32, (STEPS, frames_total), 0)
    selector = (frame_slot == (frame_index[0] + segment_slot) % frames_total).astype(jnp.float32)
    chosen = jnp.einsum("sf,fjc->sjc", selector, mri_frames, precision=lax.Precision.HIGHEST)
    partial_terms = jnp.einsum("kjc,sjc->sk", pod_basis, chosen, precision=lax.Precision.HIGHEST)
    coefficients = lax.psum(partial_terms, "ax")
    local_inflow = jnp.einsum(
        "kjc,sk->sjc", pod_basis, coefficients, precision=lax.Precision.HIGHEST
    )
    whole_inflow = lax.all_gather(local_inflow, "ax", axis=2, tiled=True)
    position = lax.axis_index("ax")
    axis_count = lax.axis_size("ax")
    height = populations.shape[2]
    plane_width = populations.shape[3]
    for segment_index in range(STEPS):
        relaxed = collide(populations, solid_mask)
        inlet_ghost = inlet_plane(
            inflow_scale * whole_inflow[segment_index], inlet_cells, height, plane_width
        )
        ghost_low, ghost_high = neighbour_planes(relaxed)
        ghost_low = jnp.where(position == 0, inlet_ghost, ghost_low)
        ghost_high = jnp.where(position == axis_count - 1, relaxed[:, -1], ghost_high)
        populations = stream(relaxed, ghost_low, ghost_high, link_flags, solid_mask)
    return (populations, local_inflow)


def solution(mesh):
    in_specs = (
        P(None, "ax", "case", None),
        P("ax", "case", None),
        P(None, "ax", "case", None),
        P("case"),
        P(None, None, "ax"),
        P(None, "case", "ax"),
        P(),
    )
    out_specs = (P(None, "ax", "case", None), P(None, "case", "ax"))
    return jax.shard_map(body, mesh=mesh, in_specs=in_specs, out_specs=out_specs, check_vma=False)
```

profile of v0, /device:TPU:1, one launch (start us, length us, event | category | flops | bytes accessed | tf_op | source)
XLA Modules:
  0.0 146.1 jit_solution(2449302820524212767)
XLA Ops:
  0.6 0.9 broadcast_compare_fusion
  1.6 3.0 %fusion.4 = f32[10,2,64,128]{3,0,2,1:T(8,128)S(1)} fusion(f32[10,19,1,1]{1,0,3,2:T(8,128)} %constant.81, f32[19,2,64,128]{3,2,1,0:T(8,128)} %param.19), kind=kOutput, calls=%fused_computation.12 | convolution fusion | flops 37355520 | bytes 1901304 | tf_op jit(solution)/shard_map/mi,i...->m.../dot_general | solution.py:74
  4.6 0.2 multiply_reduce_fusion.3
  4.9 1.5 %fusion.149 = f32[19,2,64,128]{3,0,2,1:T(8,128)S(1)} fusion(f32[19,3,1,1]{0,1,3,2:T(4,128)S(1)} %copy-done.22, f32[10,2,64,128]{3,0,2,1:T(8,128)S(1)} %fusion.4, f32[2,64,128]{2,1,0:T(8,128)S(1)} %bitcast.600), kind=kOutput, calls=%fused_computation.338 | convolution fusion | flops 11255808 | bytes 1574912 | tf_op jit(solution)/shard_map/iq,q...->i.../dot_general | solution.py:64
  6.4 0.4 copy_multiply_fusion.2
  6.8 0.8 copy-done.3
  7.7 2.8 %copy_subtract_fusion = f32[19,2,64,128]{3,0,2,1:T(8,128)S(1)} fusion(f32[19,2,64,128]{3,2,1,0:T(8,128)S(1)} %copy-done.3, f32[19,2,64,128]{3,2,1,0:T(8,128)S(1)} %get-tuple-element.100, f32[19,2,64,128]{3,2,1,0:T(8,128)S(1)} %get-tuple-element.61, f32[19,2,64,128]{3,0,2,1:T(8,128)S(1)} %fusion.149, f32[19,2,64,128]{3,2,1,0:T(8,128)S(1)} %get-tuple-element.60, ...), kind=kLoop, calls=%fused_computation.11 | loop fusion | flops 1556480 | bytes 7536640 | tf_op jit(solution)/shard_map/sub | solution.py:79
  10.5 0.9 fusion.171
  11.5 0.3 fusion.170
  11.9 1.0 subtract_select_fusion
  12.8 0.2 copy.143
  13.1 0.9 copy-done.5
  14.1 2.1 %collective-permute-start.1 = (f32[19,1,64,128]{3,2,1,0:T(8,128)S(1)}, f32[19,1,64,128]{3,2,1,0:T(8,128)}, u32[]{:S(2)}, u32[]{:S(2)}) collective-permute-start(f32[19,1,64,128]{3,2,1,0:T(8,128)S(1)} %slice.827), channel_id=1, source_target_pairs={{1,0},{2,1},{3,2},{4,3},{5,4},{6,5},{7,6},{8,7},{9,8},{10,9},{11,1... | collective-permute-start | bytes 1867784 | tf_op jit(solution)/shard_map/ppermute | solution.py:45
  16.1 0.6 slice_bitcast_fusion.36
  17.5 0.2 fusion.141
  17.7 0.3 convolution_bitcast_fusion
  18.0 31.4 %psum.7 = f32[2,512]{1,0:T(2,128)S(1)} all-reduce(f32[2,512]{1,0:T(2,128)S(1)} %convolution_bitcast_fusion), channel_id=1, replica_groups=mesh['case'=2,'ax'=16] {'ax'}, use_global_device_ids=true, to_apply=%region_1.2 | all-reduce | flops 1024 | bytes 8192 | tf_op jit(solution)/shard_map/psum | solution.py:134
  49.3 1.0 fusion.139
  50.4 0.5 compare_select_fusion
  50.9 0.8 copy.150
  51.7 23.9 %all_gather.3 = f32[2,3,512]{1,0,2:T(2,128)S(1)} all-gather(f32[2,3,32]{1,0,2:T(2,128)S(1)} %copy.150), channel_id=1, replica_groups=mesh['case'=2,'ax'=16] {'ax'}, dimensions={2}, use_global_device_ids=true | all-gather | bytes 13056 | tf_op jit(solution)/shard_map/all_gather | solution.py:138
  75.6 1.4 slice_multiply_fusion
  77.1 0.6 constant_dynamic-update-slice_fusion.17
  77.7 0.6 copy-done.9
  78.3 0.7 slice.815
  79.0 4.3 %scatter_custom_fusion = f32[3,8192]{0,1:T(8,128)} fusion(s32[512]{0:T(512)} %compare_select_fusion, f32[512,3]{1,0:T(8,128)} %bitcast.636, f32[]{:T(128)} %constant.31.clone.1), kind=kCustom, calls=%fused_computation.7 | custom fusion | bytes 98816 | tf_op jit(solution)/shard_map/scatter | solution.py:115
  83.4 3.4 %multiply_reduce_fusion.1 = f32[8192]{0:T(1024)S(1)} fusion(f32[3,8192]{0,1:T(8,128)} %scatter_custom_fusion), kind=kLoop, calls=%fused_computation.3 | loop fusion | flops 40960 | bytes 131072 | tf_op jit(solution)/shard_map/reduce_sum | solution.py:65
  86.7 0.6 constant_dynamic-update-slice_fusion.16
  87.4 0.6 constant_dynamic-update-slice_fusion.15
  88.0 0.6 multiply_bitcast_fusion.3
  88.6 4.3 %scatter_custom_fusion.1 = f32[3,8192]{0,1:T(8,128)} fusion(s32[512]{0:T(512)} %compare_select_fusion, f32[512,3]{1,0:T(8,128)} %bitcast.635, f32[]{:T(128)} %constant.31.clone.1), kind=kCustom, calls=%fused_computation.5 | custom fusion | bytes 98816 | tf_op jit(solution)/shard_map/scatter | solution.py:115
  92.9 3.5 %multiply_reduce_fusion = f32[8192]{0:T(1024)S(1)} fusion(f32[3,8192]{0,1:T(8,128)} %scatter_custom_fusion.1), kind=kLoop, calls=%fused_computation.2 | loop fusion | flops 40960 | bytes 131072 | tf_op jit(solution)/shard_map/reduce_sum | solution.py:65
  96.4 4.6 %fusion.172 = f32[19,64,128]{2,0,1:T(8,128)} fusion(f32[19,3,1]{0,1,2:T(4,128)S(1)} %copy-done.24, f32[3,64,128]{0,2,1:T(8,128)S(1)} %bitcast.598), kind=kOutput, calls=%fused_computation.343 | convolution fusion | flops 5603328 | bytes 721124 | tf_op jit(solution)/shard_map/iq,q...->i.../dot_general | solution.py:64
  101.0 2.0 %bitcast_select_fusion = (f32[19,1,64,128]{3,2,1,0:T(8,128)S(1)}, f32[19,1,64,128]{3,2,1,0:T(8,128)}) fusion(f32[19,1,64,128]{3,2,1,0:T(8,128)} %collective-permute-done.1, pred[]{:T(512)S(6)} %eq.197, f32[19,2,64,128]{3,2,1,0:T(8,128)S(1)} %copy.143), kind=kLoop, calls=%fused_computation.45 | loop fusion | flops 155648 | bytes 2490369 | tf_op jit(solution)/shard_map/jit(_where)/select_n | solution.py:150
  103.1 3.9 %collective-permute-start = (f32[19,1,64,128]{3,2,1,0:T(8,128)}, f32[19,1,64,128]{3,2,1,0:T(8,128)}, u32[]{:S(2)}, u32[]{:S(2)}) collective-permute-start(f32[19,1,64,128]{3,2,1,0:T(8,128)} %get-tuple-element.80), channel_id=1, source_target_pairs={{0,1},{1,2},{2,3},{3,4},{4,5},{5,6},{6,7},{7,8},{8,9},{9,10},{10,1... | collective-permute-start | bytes 1867784 | tf_op jit(solution)/shard_map/ppermute | solution.py:44
  107.0 1.7 %slice.867 = f32[1,2,64,128]{3,0,2,1:T(1,128)} slice(f32[19,2,64,128]{3,0,2,1:T(8,128)} %copy-done.5), slice={[18:19], [0:2], [0:64], [0:128]} | slice | bytes 131072 | tf_op jit(solution)/shard_map/slice | solution.py:109
  108.8 0.6 slice.822
  109.3 0.6 slice.821
  110.0 0.9 constant_dynamic-update-slice_fusion.14
  110.9 5.6 %fusion.173 = f32[19,64,128]{2,0,1:T(8,128)S(1)} fusion(f32[19,3,1]{0,1,2:T(4,128)} %constant.84, f32[3,64,128]{0,2,1:T(8,128)} %bitcast.597), kind=kOutput, calls=%fused_computation.344 | convolution fusion | flops 5603328 | bytes 721124 | tf_op jit(solution)/shard_map/iq,q...->i.../dot_general | solution.py:64
  116.5 1.3 fusion.19
  118.4 0.1 slice_maximum_fusion.7
  118.7 0.1 constant_dynamic-update-slice_fusion.10
  118.9 0.1 constant_dynamic-update-slice_fusion.9
  119.2 0.1 constant_dynamic-update-slice_fusion.7
  119.3 0.1 constant_dynamic-update-slice_fusion.6
  119.4 0.1 constant_dynamic-update-slice_fusion.5
  119.6 0.4 copy-done.7
  120.2 1.7 %fusion.8 = f32[10,2,64,128]{3,0,2,1:T(8,128)S(1)} fusion(f32[10,19,1,1]{1,0,3,2:T(8,128)S(1)} %copy-done.19, f32[19,2,64,128]{3,2,1,0:T(8,128)S(1)} %get-tuple-element.2), kind=kOutput, calls=%fused_computation.16 | convolution fusion | flops 37355520 | bytes 1901304 | tf_op jit(solution)/shard_map/mi,i...->m.../dot_general | solution.py:74
  121.9 0.2 multiply_reduce_fusion.2
  122.2 1.5 %fusion.150 = f32[19,2,64,128]{3,0,2,1:T(8,128)S(1)} fusion(f32[19,3,1,1]{0,1,3,2:T(4,128)S(1)} %copy-done.23, f32[10,2,64,128]{3,0,2,1:T(8,128)S(1)} %fusion.8, f32[2,64,128]{2,1,0:T(8,128)S(1)} %bitcast.604), kind=kOutput, calls=%fused_computation.339 | convolution fusion | flops 11255808 | bytes 1574912 | tf_op jit(solution)/shard_map/iq,q...->i.../dot_general | solution.py:64
  123.7 0.4 fusion.14
  124.2 0.2 copy-done.21
  124.4 1.6 %fusion.6 = f32[6,2,64,128]{3,0,2,1:T(8,128)S(1)} fusion(f32[6,19,1,1]{1,0,3,2:T(8,128)S(1)} %copy-done.21, f32[19,2,64,128]{3,2,1,0:T(8,128)S(1)} %fusion.14), kind=kOutput, calls=%fused_computation.14 | convolution fusion | flops 22413312 | bytes 1638856 | tf_op jit(solution)/shard_map/mi,i...->m.../dot_general | solution.py:80
  126.0 0.3 fusion.169
  126.4 0.3 subtract_select_fusion.1
  126.8 2.3 %collective-permute-start.2 = (f32[19,1,64,128]{3,2,0,1:T(8,128)S(1)}, f32[19,1,64,128]{3,2,0,1:T(8,128)S(1)}, u32[]{:S(2)}, u32[]{:S(2)}) collective-permute-start(f32[19,1,64,128]{3,2,0,1:T(8,128)S(1)} %get-tuple-element.67), channel_id=1, source_target_pairs={{0,1},{1,2},{2,3},{3,4},{4,5},{5,6},{6,7},{7,8},{8,9},{9,10},{10,1... | collective-permute-start | bytes 1867784 | tf_op jit(solution)/shard_map/ppermute | solution.py:44
  129.2 0.1 slice_bitcast_fusion.17
  129.6 2.1 %collective-permute-start.3 = (f32[19,1,64,128]{3,2,0,1:T(8,128)S(1)}, f32[19,1,64,128]{3,2,0,1:T(8,128)S(1)}, u32[]{:S(2)}, u32[]{:S(2)}) collective-permute-start(f32[19,1,64,128]{3,2,0,1:T(8,128)S(1)} %get-tuple-element.66), channel_id=1, source_target_pairs={{1,0},{2,1},{3,2},{4,3},{5,4},{6,5},{7,6},{8,7},{9,8},{10,9},{11,1... | collective-permute-start | bytes 1867784 | tf_op jit(solution)/shard_map/ppermute | solution.py:45
  131.7 11.2 %collective-permute-done.2 = f32[19,1,64,128]{3,2,0,1:T(8,128)S(1)} collective-permute-done((f32[19,1,64,128]{3,2,0,1:T(8,128)S(1)}, f32[19,1,64,128]{3,2,0,1:T(8,128)S(1)}, u32[]{:S(2)}, u32[]{:S(2)}) %collective-permute-start.2) | collective-permute-done | bytes 622624 | tf_op jit(solution)/shard_map/ppermute | solution.py:44
  142.9 0.2 fusion.24
  143.8 0.1 slice_maximum_fusion.3
  144.1 0.1 slice_maximum_fusion
  145.1 1.0 copy-done.27
  (140 shorter events, 3.7 us)
Async XLA Ops:
  0.6 17.1 %copy-start = (f32[512,3,32]{0,2,1:T(8,128)S(1)}, f32[512,3,32]{0,2,1:T(8,128)}, u32[]{:S(2)}) copy-start(f32[512,3,32]{0,2,1:T(8,128)} %param.23) | copy-start | bytes 589828
  1.5 3.3 %copy-start.22 = (f32[19,3,1,1]{0,1,3,2:T(4,128)S(1)}, f32[19,3,1,1]{0,1,3,2:T(4,128)}, u32[]{:S(2)}) copy-start(f32[19,3,1,1]{0,1,3,2:T(4,128)} %constant.82) | copy-start | bytes 688
  4.8 1.5 %copy-start.25 = (f32[19]{0:T(128)S(1)}, f32[19]{0:T(128)}, u32[]{:S(2)}) copy-start(f32[19]{0:T(128)} %constant.24.clone) | copy-start | bytes 232
  6.4 1.3 copy-start.3
  7.7 2.8 %copy-start.20 = (f32[6,19,1,1]{1,0,3,2:T(8,128)S(1)}, f32[6,19,1,1]{1,0,3,2:T(8,128)}, u32[]{:S(2)}) copy-start(f32[6,19,1,1]{1,0,3,2:T(8,128)} %constant.83) | copy-start | bytes 1372
  12.8 1.2 copy-start.5
  14.0 3.5 %copy-start.29 = (f32[24,3,32]{2,0,1:T(8,128)S(1)}, f32[24,3,32]{2,0,1:T(8,128)}, u32[]{:S(2)}) copy-start(f32[24,3,32]{2,0,1:T(8,128)} %param.24) | copy-start | bytes 27652
  14.0 36.4 %copy-start.28 = (s32[512]{0:T(512)S(1)}, s32[512]{0:T(512)}, u32[]{:S(2)}) copy-start(s32[512]{0:T(512)} %param.22) | copy-start | bytes 6148
  14.1 87.0 %collective-permute-start.1 = (f32[19,1,64,128]{3,2,1,0:T(8,128)S(1)}, f32[19,1,64,128]{3,2,1,0:T(8,128)}, u32[]{:S(2)}, u32[]{:S(2)}) collective-permute-start(f32[19,1,64,128]{3,2,1,0:T(8,128)S(1)} %slice.827), channel_id=1, source_target_pairs={{1,0},{2,1},{3,2},{4,3},{5,4},{6,5},{7,6},{8,7},{9,8},{10,9},{11,1... | collective-permute-start | bytes 1867784 | tf_op jit(solution)/shard_map/ppermute | solution.py:45
  16.8 60.3 %copy-start.1 = (s32[2,64,128]{2,1,0:T(8,128)S(1)}, s32[2,64,128]{2,1,0:T(8,128)}, u32[]{:S(2)}) copy-start(s32[2,64,128]{2,1,0:T(8,128)} %param.20) | copy-start | bytes 196612
  16.8 60.3 %copy-start.4 = (s32[2,2,64,128]{3,2,1,0:T(8,128)S(1)}, s32[2,2,64,128]{3,2,1,0:T(8,128)}, u32[]{:S(2)}) copy-start(s32[2,2,64,128]{3,2,1,0:T(8,128)} %param.21) | copy-start | bytes 393220
  51.7 25.3 %copy-start.8 = (f32[2,64,128]{2,1,0:T(8,128)S(1)}, f32[2,64,128]{2,1,0:T(8,128)}, u32[]{:S(2)}) copy-start(f32[2,64,128]{2,1,0:T(8,128)} %get-tuple-element.84) | copy-start | bytes 196612
  77.7 0.6 copy-start.9
  77.7 1.3 copy-start.12
  83.3 3.4 %copy-start.10 = (f32[2,64,128]{2,1,0:T(8,128)S(1)}, f32[2,64,128]{2,1,0:T(8,128)}, u32[]{:S(2)}) copy-start(f32[2,64,128]{2,1,0:T(8,128)} %copy-done.9) | copy-start | bytes 196612
  83.3 3.4 %copy-start.14 = (f32[2,64,127]{2,1,0:T(8,128)S(1)}, f32[2,64,127]{2,1,0:T(8,128)}, u32[]{:S(2)}) copy-start(f32[2,64,127]{2,1,0:T(8,128)} %slice.815) | copy-start | bytes 195076
  83.3 4.0 %copy-start.13 = (f32[2,64,128]{2,1,0:T(8,128)S(1)}, f32[2,64,128]{2,1,0:T(8,128)}, u32[]{:S(2)}) copy-start(f32[2,64,128]{2,1,0:T(8,128)} %copy-done.12) | copy-start | bytes 196612
  92.9 3.5 %copy-start.2 = (f32[3,8192]{0,1:T(8,128)S(1)}, f32[3,8192]{0,1:T(8,128)}, u32[]{:S(2)}) copy-start(f32[3,8192]{0,1:T(8,128)} %scatter_custom_fusion) | copy-start | bytes 294916
  92.9 3.5 %copy-start.24 = (f32[19,3,1]{0,1,2:T(4,128)S(1)}, f32[19,3,1]{0,1,2:T(4,128)}, u32[]{:S(2)}) copy-start(f32[19,3,1]{0,1,2:T(4,128)} %constant.84) | copy-start | bytes 688
  101.0 7.7 %copy-start.11 = (f32[2,64,128]{2,1,0:T(8,128)S(1)}, f32[2,64,128]{2,1,0:T(8,128)}, u32[]{:S(2)}) copy-start(f32[2,64,128]{2,1,0:T(8,128)} %get-tuple-element.81) | copy-start | bytes 196612
  103.1 13.4 %collective-permute-start = (f32[19,1,64,128]{3,2,1,0:T(8,128)}, f32[19,1,64,128]{3,2,1,0:T(8,128)}, u32[]{:S(2)}, u32[]{:S(2)}) collective-permute-start(f32[19,1,64,128]{3,2,1,0:T(8,128)} %get-tuple-element.80), channel_id=1, source_target_pairs={{0,1},{1,2},{2,3},{3,4},{4,5},{5,6},{6,7},{7,8},{8,9},{9,10},{10,1... | collective-permute-start | bytes 1867784 | tf_op jit(solution)/shard_map/ppermute | solution.py:44
  110.9 5.6 %copy-start.6 = (f32[19,64,128]{2,0,1:T(8,128)S(1)}, f32[19,64,128]{2,0,1:T(8,128)}, u32[]{:S(2)}) copy-start(f32[19,64,128]{2,0,1:T(8,128)} %fusion.172) | copy-start | bytes 1867780
  110.9 5.6 %copy-start.15 = (f32[64,128]{1,0:T(8,128)S(1)}, f32[64,128]{1,0:T(8,128)}, u32[]{:S(2)}) copy-start(f32[64,128]{1,0:T(8,128)} %multiply_bitcast_fusion.3) | copy-start | bytes 98308
  110.9 5.6 %copy-start.26 = (f32[19]{0:T(128)S(1)}, f32[19]{0:T(128)}, u32[]{:S(2)}) copy-start(f32[19]{0:T(128)} %constant.24.clone) | copy-start | bytes 232
  119.2 0.8 copy-start.7
  119.4 0.8 copy-start.19
  120.2 2.0 %copy-start.23 = (f32[19,3,1,1]{0,1,3,2:T(4,128)S(1)}, f32[19,3,1,1]{0,1,3,2:T(4,128)}, u32[]{:S(2)}) copy-start(f32[19,3,1,1]{0,1,3,2:T(4,128)} %constant.82) | copy-start | bytes 688
  123.7 0.7 copy-start.21
  126.7 2.5 %copy-start.16 = (pred[2,64,128]{2,1,0:T(8,128)(4,1)S(1)}, pred[2,64,128]{2,1,0:T(8,128)(4,1)}, u32[]{:S(2)}) copy-start(pred[2,64,128]{2,1,0:T(8,128)(4,1)} %get-tuple-element.37) | copy-start | bytes 49156
  126.7 2.7 %copy-start.18 = (pred[2,64,128]{2,1,0:T(8,128)(4,1)S(1)}, pred[2,64,128]{2,1,0:T(8,128)(4,1)}, u32[]{:S(2)}) copy-start(pred[2,64,128]{2,1,0:T(8,128)(4,1)} %get-tuple-element.35) | copy-start | bytes 49156
  126.8 2.7 %copy-start.17 = (pred[2,64,128]{2,1,0:T(8,128)(4,1)S(1)}, pred[2,64,128]{2,1,0:T(8,128)(4,1)}, u32[]{:S(2)}) copy-start(pred[2,64,128]{2,1,0:T(8,128)(4,1)} %get-tuple-element.33) | copy-start | bytes 49156
  126.8 16.1 %collective-permute-start.2 = (f32[19,1,64,128]{3,2,0,1:T(8,128)S(1)}, f32[19,1,64,128]{3,2,0,1:T(8,128)S(1)}, u32[]{:S(2)}, u32[]{:S(2)}) collective-permute-start(f32[19,1,64,128]{3,2,0,1:T(8,128)S(1)} %get-tuple-element.67), channel_id=1, source_target_pairs={{0,1},{1,2},{2,3},{3,4},{4,5},{5,6},{6,7},{7,8},{8,9},{9,10},{10,1... | collective-permute-start | bytes 1867784 | tf_op jit(solution)/shard_map/ppermute | solution.py:44
  129.6 13.7 %collective-permute-start.3 = (f32[19,1,64,128]{3,2,0,1:T(8,128)S(1)}, f32[19,1,64,128]{3,2,0,1:T(8,128)S(1)}, u32[]{:S(2)}, u32[]{:S(2)}) collective-permute-start(f32[19,1,64,128]{3,2,0,1:T(8,128)S(1)} %get-tuple-element.66), channel_id=1, source_target_pairs={{1,0},{2,1},{3,2},{4,3},{5,4},{6,5},{7,6},{8,7},{9,8},{10,9},{11,1... | collective-permute-start | bytes 1867784 | tf_op jit(solution)/shard_map/ppermute | solution.py:45
  145.1 1.0 copy-start.27
where the time goes:
time: 147 us; the launch traced here: 146 us
  blocking collectives  55.3 us (38%)
  other arithmetic  25.1 us (17%)
  matrix products  21.8 us (15%)
  local copies, waits for them, and re-layouts  20 us (14%)
  waiting for transfers between devices  11.2 us (8%)
  starting transfers between devices  10.4 us (7%)
  between operations  2.29 us (2%)
    psum x1, blocking collectives, body(): coefficients = lax.psum(partial_terms, 'ax')  31.4 us
    all_gather x1, blocking collectives, body(): whole_inflow = lax.all_gather(local_inflow, 'ax', axis=2, tiled=True)  23.9 us
    dot_general x4, matrix products, equilibrium(): jnp.einsum('iq,q...->i...', lattice, velocity, precision=lax.Precision.HI...  13.1 us
    ppermute x2, waiting for transfers between devices, extended(): before = lax.ppermute(last, axis, up)  11.2 us
    scatter x2, local copies, waits for them, and re-layouts, inlet_plane(): jnp.zeros((3, height * plane_width), jnp.float32).at[:, inlet_cells]  8.61 us
    reduce_sum x4, other arithmetic, equilibrium(): speed_sq = jnp.sum(velocity * velocity, axis=0)  7.34 us
    ppermute x2, starting transfers between devices, extended(): before = lax.ppermute(last, axis, up)  6.2 us
    dot_general x2, matrix products, collide(): jnp.einsum('mi,i...->m...', moment_rows(), populations, precision=lax.Pre...  4.7 us
  transfers between devices with their start and end apart: 4, of which 1 were waited for; matrix products, arithmetic and copies ran while one was open for 26% of the time, Pallas kernels for 0%

commit v1 on v0

--- a/solution.py
+++ b/solution.py
@@ -135,7 +135,16 @@
     local_inflow = jnp.einsum(
         "kjc,sk->sjc", pod_basis, coefficients, precision=lax.Precision.HIGHEST
     )
-    whole_inflow = lax.all_gather(local_inflow, "ax", axis=2, tiled=True)
+    array_2 = local_inflow
+    ways, here, step = (lax.axis_size("ax"), lax.axis_index("ax"), array_2.shape[2])
+    lengths = [n * ways if d == 2 else n for d, n in enumerate(array_2.shape)]
+    full = lax.dynamic_update_slice_in_dim(
+        jnp.zeros(lengths, array_2.dtype), array_2, here * step, axis=2
+    )
+    for far in range(1, ways):
+        array_2 = lax.ppermute(array_2, "ax", [(d, (d + 1) % ways) for d in range(ways)])
+        full = lax.dynamic_update_slice_in_dim(full, array_2, (here - far) % ways * step, axis=2)
+    whole_inflow = full
     position = lax.axis_index("ax")
     axis_count = lax.axis_size("ax")
     height = populations.shape[2]

time: 147 us -> 198 us (1.35)
  waiting for transfers between devices: 11.2 us -> 90.5 us
  blocking collectives: 55.3 us -> 31.5 us
  local copies, waits for them, and re-layouts: 20 us -> 12.6 us
  other arithmetic: 25.1 us -> 28.9 us
  matrix products: 21.8 us -> 19.2 us
  starting transfers between devices: 10.4 us -> 12.5 us
    ppermute x0 -> x15, waiting for transfers between devices: none -> 78.1 us  [body(): lax.ppermute(array_2, 'ax', [(d, (d + 1) % ways) for d in range(ways)])]
    all_gather x1 -> x0, blocking collectives: 23.9 us -> none  [body(): whole_inflow = lax.all_gather(local_inflow, 'ax', axis=2, tiled=True)]
    scatter x2 -> x0, local copies, waits for them, and re-layouts: 8.61 us -> none  [inlet_plane(): jnp.zeros((3, height * plane_width), jnp.float32).at[:, inlet_cells]]
    scatter x0 -> x2, other arithmetic: none -> 8.13 us  [inlet_plane(): jnp.zeros((3, height * plane_width), jnp.float32).at[:, inlet_cells]]
    dot_general x4, matrix products: 13.1 us -> 10.5 us  [equilibrium(): jnp.einsum('iq,q...->i...', lattice, velocity, precision=lax.Precision.HI...]
    ppermute x0 -> x15, starting transfers between devices: none -> 2.09 us  [body(): lax.ppermute(array_2, 'ax', [(d, (d + 1) % ways) for d in range(ways)])]
    ppermute x0 -> x15, local copies, waits for them, and re-layouts: none -> 2.04 us  [body(): lax.ppermute(array_2, 'ax', [(d, (d + 1) % ways) for d in range(ways)])]
    unnamed x61 -> x45, local copies, waits for them, and re-layouts: 4.29 us -> 3.54 us
  transfers between devices with their start and end apart: 4 -> 19, of which waited for: 1 -> 17; matrix products, arithmetic and copies ran while one was open for 26% -> 18% of each run, Pallas kernels for 0% -> 0%
where the time goes in v1:
time: 198 us
  waiting for transfers between devices  90.5 us (46%)
  blocking collectives  31.5 us (16%)
  other arithmetic  28.9 us (15%)
  matrix products  19.2 us (10%)
  local copies, waits for them, and re-layouts  12.6 us (6%)
  starting transfers between devices  12.5 us (6%)
  between operations  2.45 us (1%)
    ppermute x15, waiting for transfers between devices, body(): lax.ppermute(array_2, 'ax', [(d, (d + 1) % ways) for d in range(ways)])  78.1 us
    psum x1, blocking collectives, body(): coefficients = lax.psum(partial_terms, 'ax')  31.5 us
    ppermute x2, waiting for transfers between devices, extended(): before = lax.ppermute(last, axis, up)  11.6 us
    dot_general x4, matrix products, equilibrium(): jnp.einsum('iq,q...->i...', lattice, velocity, precision=lax.Precision.HI...  10.5 us
    scatter x2, other arithmetic, inlet_plane(): jnp.zeros((3, height * plane_width), jnp.float32).at[:, inlet_cells]  8.13 us
    reduce_sum x4, other arithmetic, equilibrium(): speed_sq = jnp.sum(velocity * velocity, axis=0)  7.3 us
    ppermute x2, starting transfers between devices, extended(): before = lax.ppermute(last, axis, up)  6.53 us
    unnamed x28, other arithmetic  4.96 us
  transfers between devices with their start and end apart: 19, of which 17 were waited for; matrix products, arithmetic and copies ran while one was open for 18% of the time, Pallas kernels for 0%

profile of v1, /device:TPU:1, one launch (start us, length us, event | category | flops | bytes accessed | tf_op | source)
XLA Modules:
  0.0 197.5 jit_solution(1939012870211484256)
XLA Ops:
  0.7 3.0 %fusion.4 = f32[10,2,64,128]{3,0,2,1:T(8,128)S(1)} fusion(f32[10,19,1,1]{1,0,3,2:T(8,128)} %constant.197, f32[19,2,64,128]{3,2,1,0:T(8,128)} %param.19), kind=kOutput, calls=%fused_computation.12 | convolution fusion | flops 37355520 | bytes 1901304 | tf_op jit(solution)/shard_map/mi,i...->m.../dot_general | solution.py:74
  3.7 0.2 multiply_reduce_fusion.3
  4.0 1.5 fusion.155
  5.5 0.4 copy_multiply_fusion.2
  6.0 0.8 copy-done.4
  6.8 2.8 %copy_subtract_fusion = f32[19,2,64,128]{3,0,2,1:T(8,128)S(1)} fusion(f32[19,2,64,128]{3,2,1,0:T(8,128)S(1)} %copy-done.4, f32[19,2,64,128]{3,2,1,0:T(8,128)S(1)} %get-tuple-element.98, f32[19,2,64,128]{3,2,1,0:T(8,128)S(1)} %get-tuple-element.61, f32[19,2,64,128]{3,0,2,1:T(8,128)S(1)} %fusion.155, f32[19,2,64,128]{3,2,1,0:T(8,128)S(1)} %get-tuple-element.60, ...), kind=kLoop, calls=%fused_computation.11 | loop fusion | flops 1556480 | bytes 7536640 | tf_op jit(solution)/shard_map/sub | solution.py:79
  9.7 0.9 fusion.177
  10.6 0.3 fusion.176
  11.0 1.0 subtract_select_fusion
  12.0 0.2 copy.105
  12.3 0.9 copy-done.6
  13.2 0.9 slice.827
  14.1 1.9 collective-permute-start.16
  16.9 0.3 convolution_bitcast_fusion
  17.1 31.5 %psum.7 = f32[2,512]{1,0:T(2,128)S(1)} all-reduce(f32[2,512]{1,0:T(2,128)S(1)} %convolution_bitcast_fusion), channel_id=1, replica_groups=mesh['case'=2,'ax'=16] {'ax'}, use_global_device_ids=true, to_apply=%region_1.2 | all-reduce | flops 1024 | bytes 8192 | tf_op jit(solution)/shard_map/psum | solution.py:134
  48.6 1.0 fusion.145
  49.6 1.6 collective-permute-start
  51.3 1.4 copy.112
  52.8 0.6 constant_dynamic-update-slice_fusion.17
  53.5 0.6 constant_dynamic-update-slice_fusion.16
  54.1 0.6 constant_dynamic-update-slice_fusion.15
  54.8 0.6 slice.822
  55.3 1.1 slice.867
  56.5 0.6 compare_select_fusion
  57.1 0.8 constant_dynamic-update-slice_fusion.53
  57.9 1.3 constant_dynamic-update-slice_fusion.14
  59.2 0.7 copy.113
  60.0 4.1 %collective-permute-done.1 = f32[2,3,32]{2,0,1:T(2,128)S(1)} collective-permute-done((f32[2,3,32]{2,0,1:T(2,128)}, f32[2,3,32]{2,0,1:T(2,128)S(1)}, u32[]{:S(2)}, u32[]{:S(2)}) %collective-permute-start.1) | collective-permute-done | bytes 800 | tf_op jit(solution)/shard_map/ppermute | solution.py:145
  64.2 5.7 %collective-permute-done.2 = f32[2,3,32]{2,0,1:T(2,128)S(1)} collective-permute-done((f32[2,3,32]{2,0,1:T(2,128)S(1)}, f32[2,3,32]{2,0,1:T(2,128)S(1)}, u32[]{:S(2)}, u32[]{:S(2)}) %collective-permute-start.2) | collective-permute-done | bytes 800 | tf_op jit(solution)/shard_map/ppermute | solution.py:145
  70.1 5.7 %collective-permute-done.3 = f32[2,3,32]{2,0,1:T(2,128)S(1)} collective-permute-done((f32[2,3,32]{2,0,1:T(2,128)S(1)}, f32[2,3,32]{2,0,1:T(2,128)S(1)}, u32[]{:S(2)}, u32[]{:S(2)}) %collective-permute-start.3) | collective-permute-done | bytes 800 | tf_op jit(solution)/shard_map/ppermute | solution.py:145
  75.9 5.7 %collective-permute-done.4 = f32[2,3,32]{2,0,1:T(2,128)S(1)} collective-permute-done((f32[2,3,32]{2,0,1:T(2,128)S(1)}, f32[2,3,32]{2,0,1:T(2,128)S(1)}, u32[]{:S(2)}, u32[]{:S(2)}) %collective-permute-start.4) | collective-permute-done | bytes 800 | tf_op jit(solution)/shard_map/ppermute | solution.py:145
  81.9 5.7 %collective-permute-done.5 = f32[2,3,32]{2,0,1:T(2,128)S(1)} collective-permute-done((f32[2,3,32]{2,0,1:T(2,128)S(1)}, f32[2,3,32]{2,0,1:T(2,128)S(1)}, u32[]{:S(2)}, u32[]{:S(2)}) %collective-permute-start.5) | collective-permute-done | bytes 800 | tf_op jit(solution)/shard_map/ppermute | solution.py:145
  87.7 5.7 %collective-permute-done.6 = f32[2,3,32]{2,0,1:T(2,128)S(1)} collective-permute-done((f32[2,3,32]{2,0,1:T(2,128)S(1)}, f32[2,3,32]{2,0,1:T(2,128)S(1)}, u32[]{:S(2)}, u32[]{:S(2)}) %collective-permute-start.6) | collective-permute-done | bytes 800 | tf_op jit(solution)/shard_map/ppermute | solution.py:145
  93.6 5.7 %collective-permute-done.7 = f32[2,3,32]{2,0,1:T(2,128)S(1)} collective-permute-done((f32[2,3,32]{2,0,1:T(2,128)S(1)}, f32[2,3,32]{2,0,1:T(2,128)S(1)}, u32[]{:S(2)}, u32[]{:S(2)}) %collective-permute-start.7) | collective-permute-done | bytes 800 | tf_op jit(solution)/shard_map/ppermute | solution.py:145
  99.4 5.7 %collective-permute-done.8 = f32[2,3,32]{2,0,1:T(2,128)S(1)} collective-permute-done((f32[2,3,32]{2,0,1:T(2,128)S(1)}, f32[2,3,32]{2,0,1:T(2,128)S(1)}, u32[]{:S(2)}, u32[]{:S(2)}) %collective-permute-start.8) | collective-permute-done | bytes 800 | tf_op jit(solution)/shard_map/ppermute | solution.py:145
  105.2 5.7 %collective-permute-done.9 = f32[2,3,32]{2,0,1:T(2,128)S(1)} collective-permute-done((f32[2,3,32]{2,0,1:T(2,128)S(1)}, f32[2,3,32]{2,0,1:T(2,128)S(1)}, u32[]{:S(2)}, u32[]{:S(2)}) %collective-permute-start.9) | collective-permute-done | bytes 800 | tf_op jit(solution)/shard_map/ppermute | solution.py:145
  111.0 5.7 %collective-permute-done.10 = f32[2,3,32]{2,0,1:T(2,128)S(1)} collective-permute-done((f32[2,3,32]{2,0,1:T(2,128)S(1)}, f32[2,3,32]{2,0,1:T(2,128)S(1)}, u32[]{:S(2)}, u32[]{:S(2)}) %collective-permute-start.10) | collective-permute-done | bytes 800 | tf_op jit(solution)/shard_map/ppermute | solution.py:145
  116.9 5.7 %collective-permute-done.11 = f32[2,3,32]{2,0,1:T(2,128)S(1)} collective-permute-done((f32[2,3,32]{2,0,1:T(2,128)S(1)}, f32[2,3,32]{2,0,1:T(2,128)S(1)}, u32[]{:S(2)}, u32[]{:S(2)}) %collective-permute-start.11) | collective-permute-done | bytes 800 | tf_op jit(solution)/shard_map/ppermute | solution.py:145
  122.7 5.7 %collective-permute-done.12 = f32[2,3,32]{2,0,1:T(2,128)S(1)} collective-permute-done((f32[2,3,32]{2,0,1:T(2,128)S(1)}, f32[2,3,32]{2,0,1:T(2,128)S(1)}, u32[]{:S(2)}, u32[]{:S(2)}) %collective-permute-start.12) | collective-permute-done | bytes 800 | tf_op jit(solution)/shard_map/ppermute | solution.py:145
  128.5 5.7 %collective-permute-done.13 = f32[2,3,32]{2,0,1:T(2,128)S(1)} collective-permute-done((f32[2,3,32]{2,0,1:T(2,128)S(1)}, f32[2,3,32]{2,0,1:T(2,128)S(1)}, u32[]{:S(2)}, u32[]{:S(2)}) %collective-permute-start.13) | collective-permute-done | bytes 800 | tf_op jit(solution)/shard_map/ppermute | solution.py:145
  134.4 5.7 %collective-permute-done.14 = f32[2,3,32]{2,0,1:T(2,128)S(1)} collective-permute-done((f32[2,3,32]{2,0,1:T(2,128)S(1)}, f32[2,3,32]{2,0,1:T(2,128)S(1)}, u32[]{:S(2)}, u32[]{:S(2)}) %collective-permute-start.14) | collective-permute-done | bytes 800 | tf_op jit(solution)/shard_map/ppermute | solution.py:145
  140.1 4.1 %scatter_custom_fusion = f32[3,8192]{0,1:T(8,128)} fusion(s32[512]{0:T(512)} %compare_select_fusion, f32[]{:T(128)} %constant.151.clone.1, f32[2,3,512]{1,2,0:T(8,128)S(1)} %constant_dynamic-update-slice_fusion.38, f32[]{:T(128)} %constant.184.clone.1), kind=kCustom, calls=%fused_computation.7 | custom fusion | flops 1536 | bytes 361472 | tf_op jit(solution)/shard_map/scatter | solution.py:115
  144.2 3.3 %multiply_reduce_fusion.1 = f32[8192]{0:T(1024)S(1)} fusion(f32[3,8192]{0,1:T(8,128)} %scatter_custom_fusion), kind=kLoop, calls=%fused_computation.3 | loop fusion | flops 40960 | bytes 131072 | tf_op jit(solution)/shard_map/reduce_sum | solution.py:65
  147.6 4.0 %scatter_custom_fusion.1 = f32[3,8192]{0,1:T(8,128)} fusion(s32[512]{0:T(512)} %compare_select_fusion, f32[]{:T(128)} %constant.151.clone.1, f32[2,3,512]{1,2,0:T(8,128)S(1)} %constant_dynamic-update-slice_fusion.38, f32[]{:T(128)} %constant.184.clone.1), kind=kCustom, calls=%fused_computation.5 | custom fusion | flops 1536 | bytes 361472 | tf_op jit(solution)/shard_map/scatter | solution.py:115
  151.6 3.5 %multiply_reduce_fusion = f32[8192]{0:T(1024)S(1)} fusion(f32[3,8192]{0,1:T(8,128)} %scatter_custom_fusion.1), kind=kLoop, calls=%fused_computation.2 | loop fusion | flops 40960 | bytes 131072 | tf_op jit(solution)/shard_map/reduce_sum | solution.py:65
  155.1 3.7 %fusion.178 = f32[19,64,128]{2,0,1:T(8,128)S(1)} fusion(f32[19,3,1]{0,1,2:T(4,128)S(1)} %copy-done.16, f32[3,64,128]{0,2,1:T(8,128)S(1)} %bitcast.600), kind=kOutput, calls=%fused_computation.363 | convolution fusion | flops 5603328 | bytes 721124 | tf_op jit(solution)/shard_map/iq,q...->i.../dot_general | solution.py:64
  158.9 1.2 bitcast_select_fusion
  160.1 2.1 %collective-permute-start.15 = (f32[19,1,64,128]{3,2,1,0:T(8,128)S(1)}, f32[19,1,64,128]{3,2,1,0:T(8,128)S(1)}, u32[]{:S(2)}, u32[]{:S(2)}) collective-permute-start(f32[19,1,64,128]{3,2,1,0:T(8,128)S(1)} %get-tuple-element.80), channel_id=1, source_target_pairs={{0,1},{1,2},{2,3},{3,4},{4,5},{5,6},{6,7},{7,8},{8,9},{9,10},{10,1... | collective-permute-start | bytes 1867784 | tf_op jit(solution)/shard_map/ppermute | solution.py:44
  162.3 3.8 %fusion.179 = f32[19,64,128]{2,0,1:T(8,128)S(1)} fusion(f32[19,3,1]{0,1,2:T(4,128)S(1)} %copy-done.16, f32[3,64,128]{0,2,1:T(8,128)S(1)} %bitcast.599), kind=kOutput, calls=%fused_computation.364 | convolution fusion | flops 5603328 | bytes 721124 | tf_op jit(solution)/shard_map/iq,q...->i.../dot_general | solution.py:64
  166.0 3.1 %collective-permute-done.15 = f32[19,1,64,128]{3,2,1,0:T(8,128)S(1)} collective-permute-done((f32[19,1,64,128]{3,2,1,0:T(8,128)S(1)}, f32[19,1,64,128]{3,2,1,0:T(8,128)S(1)}, u32[]{:S(2)}, u32[]{:S(2)}) %collective-permute-start.15) | collective-permute-done | bytes 622624 | tf_op jit(solution)/shard_map/ppermute | solution.py:44
  171.3 0.3 copy-done.11
  171.6 1.7 fusion.8
  173.4 1.5 fusion.156
  174.9 0.2 multiply_reduce_fusion.2
  175.1 0.4 fusion.14
  175.6 0.2 copy-done.13
  175.8 1.6 fusion.6
  177.4 0.3 fusion.175
  177.8 0.3 subtract_select_fusion.1
  178.3 4.4 %collective-permute-start.17 = (f32[19,1,64,128]{3,2,0,1:T(8,128)S(1)}, f32[19,1,64,128]{3,2,0,1:T(8,128)S(1)}, u32[]{:S(2)}, u32[]{:S(2)}) collective-permute-start(f32[19,1,64,128]{3,2,0,1:T(8,128)S(1)} %get-tuple-element.67), channel_id=1, source_target_pairs={{0,1},{1,2},{2,3},{3,4},{4,5},{5,6},{6,7},{7,8},{8,9},{9,10},{10,1... | collective-permute-start | bytes 1867784 | tf_op jit(solution)/shard_map/ppermute | solution.py:44
  183.1 1.9 collective-permute-start.18
  185.1 8.5 %collective-permute-done.17 = f32[19,1,64,128]{3,2,0,1:T(8,128)S(1)} collective-permute-done((f32[19,1,64,128]{3,2,0,1:T(8,128)S(1)}, f32[19,1,64,128]{3,2,0,1:T(8,128)S(1)}, u32[]{:S(2)}, u32[]{:S(2)}) %collective-permute-start.17) | collective-permute-done | bytes 622624 | tf_op jit(solution)/shard_map/ppermute | solution.py:44
  193.9 0.7 collective-permute-done.18
  196.5 1.0 copy-done.19
  (184 shorter events, 7.1 us)
Async XLA Ops:
  0.6 16.2 %copy-start = (f32[512,3,32]{0,2,1:T(8,128)S(1)}, f32[512,3,32]{0,2,1:T(8,128)}, u32[]{:S(2)}) copy-start(f32[512,3,32]{0,2,1:T(8,128)} %param.23) | copy-start | bytes 589828
  0.6 3.3 %copy-start.14 = (f32[19,3,1,1]{0,1,3,2:T(4,128)S(1)}, f32[19,3,1,1]{0,1,3,2:T(4,128)}, u32[]{:S(2)}) copy-start(f32[19,3,1,1]{0,1,3,2:T(4,128)} %constant.198) | copy-start | bytes 688
  4.0 1.5 copy-start.17
  5.5 1.3 copy-start.4
  6.8 2.8 %copy-start.12 = (f32[6,19,1,1]{1,0,3,2:T(8,128)S(1)}, f32[6,19,1,1]{1,0,3,2:T(8,128)}, u32[]{:S(2)}) copy-start(f32[6,19,1,1]{1,0,3,2:T(8,128)} %constant.199) | copy-start | bytes 1372
  9.7 1.3 copy-start.1
  12.0 1.2 copy-start.6
  13.2 3.5 %copy-start.21 = (f32[24,3,32]{2,0,1:T(8,128)S(1)}, f32[24,3,32]{2,0,1:T(8,128)}, u32[]{:S(2)}) copy-start(f32[24,3,32]{2,0,1:T(8,128)} %param.24) | copy-start | bytes 27652
  13.2 39.6 %copy-start.5 = (s32[2,2,64,128]{3,2,1,0:T(8,128)S(1)}, s32[2,2,64,128]{3,2,1,0:T(8,128)}, u32[]{:S(2)}) copy-start(s32[2,2,64,128]{3,2,1,0:T(8,128)} %param.21) | copy-start | bytes 393220
  14.1 144.8 %collective-permute-start.16 = (f32[19,1,64,128]{3,2,1,0:T(8,128)}, f32[19,1,64,128]{3,2,1,0:T(8,128)}, u32[]{:S(2)}, u32[]{:S(2)}) collective-permute-start(f32[19,1,64,128]{3,2,1,0:T(8,128)} %slice.827), channel_id=1, source_target_pairs={{1,0},{2,1},{3,2},{4,3},{5,4},{6,5},{7,6},{8,7},{9,8},{10,9},{11,1... | collective-permute-start | bytes 1867784 | tf_op jit(solution)/shard_map/ppermute | solution.py:45
  49.6 9.5 %collective-permute-start = (f32[2,3,32]{2,0,1:T(2,128)}, f32[2,3,32]{2,0,1:T(2,128)}, u32[]{:S(2)}, u32[]{:S(2)}) collective-permute-start(f32[2,3,32]{2,0,1:T(2,128)} %fusion.145), channel_id=1, source_target_pairs={{0,1},{1,2},{2,3},{3,4},{4,5},{5,6},{6,7},{7,8},{8,9},{9,10},{10,1... | collective-permute-start | bytes 2312 | tf_op jit(solution)/shard_map/ppermute | solution.py:145
  52.7 3.8 %copy-start.20 = (s32[512]{0:T(512)S(1)}, s32[512]{0:T(512)}, u32[]{:S(2)}) copy-start(s32[512]{0:T(512)} %param.22) | copy-start | bytes 6148
  59.9 4.2 %collective-permute-start.1 = (f32[2,3,32]{2,0,1:T(2,128)}, f32[2,3,32]{2,0,1:T(2,128)S(1)}, u32[]{:S(2)}, u32[]{:S(2)}) collective-permute-start(f32[2,3,32]{2,0,1:T(2,128)} %collective-permute-done), channel_id=1, source_target_pairs={{0,1},{1,2},{2,3},{3,4},{4,5},{5,6},{6,7},{7,8},{8,9},{9,10},{10,1... | collective-permute-start | bytes 2312 | tf_op jit(solution)/shard_map/ppermute | solution.py:145
  64.2 5.8 %collective-permute-start.2 = (f32[2,3,32]{2,0,1:T(2,128)S(1)}, f32[2,3,32]{2,0,1:T(2,128)S(1)}, u32[]{:S(2)}, u32[]{:S(2)}) collective-permute-start(f32[2,3,32]{2,0,1:T(2,128)S(1)} %collective-permute-done.1), channel_id=1, source_target_pairs={{0,1},{1,2},{2,3},{3,4},{4,5},{5,6},{6,7},{7,8},{8,9},{9,10},{10,1... | collective-permute-start | bytes 2312 | tf_op jit(solution)/shard_map/ppermute | solution.py:145
  70.0 5.7 %collective-permute-start.3 = (f32[2,3,32]{2,0,1:T(2,128)S(1)}, f32[2,3,32]{2,0,1:T(2,128)S(1)}, u32[]{:S(2)}, u32[]{:S(2)}) collective-permute-start(f32[2,3,32]{2,0,1:T(2,128)S(1)} %collective-permute-done.2), channel_id=1, source_target_pairs={{0,1},{1,2},{2,3},{3,4},{4,5},{5,6},{6,7},{7,8},{8,9},{9,10},{10,1... | collective-permute-start | bytes 2312 | tf_op jit(solution)/shard_map/ppermute | solution.py:145
  75.9 5.7 %collective-permute-start.4 = (f32[2,3,32]{2,0,1:T(2,128)S(1)}, f32[2,3,32]{2,0,1:T(2,128)S(1)}, u32[]{:S(2)}, u32[]{:S(2)}) collective-permute-start(f32[2,3,32]{2,0,1:T(2,128)S(1)} %collective-permute-done.3), channel_id=1, source_target_pairs={{0,1},{1,2},{2,3},{3,4},{4,5},{5,6},{6,7},{7,8},{8,9},{9,10},{10,1... | collective-permute-start | bytes 2312 | tf_op jit(solution)/shard_map/ppermute | solution.py:145
  81.7 5.9 %collective-permute-start.5 = (f32[2,3,32]{2,0,1:T(2,128)S(1)}, f32[2,3,32]{2,0,1:T(2,128)S(1)}, u32[]{:S(2)}, u32[]{:S(2)}) collective-permute-start(f32[2,3,32]{2,0,1:T(2,128)S(1)} %collective-permute-done.4), channel_id=1, source_target_pairs={{0,1},{1,2},{2,3},{3,4},{4,5},{5,6},{6,7},{7,8},{8,9},{9,10},{10,1... | collective-permute-start | bytes 2312 | tf_op jit(solution)/shard_map/ppermute | solution.py:145
  87.7 5.7 %collective-permute-start.6 = (f32[2,3,32]{2,0,1:T(2,128)S(1)}, f32[2,3,32]{2,0,1:T(2,128)S(1)}, u32[]{:S(2)}, u32[]{:S(2)}) collective-permute-start(f32[2,3,32]{2,0,1:T(2,128)S(1)} %collective-permute-done.5), channel_id=1, source_target_pairs={{0,1},{1,2},{2,3},{3,4},{4,5},{5,6},{6,7},{7,8},{8,9},{9,10},{10,1... | collective-permute-start | bytes 2312 | tf_op jit(solution)/shard_map/ppermute | solution.py:145
  93.5 5.7 %collective-permute-start.7 = (f32[2,3,32]{2,0,1:T(2,128)S(1)}, f32[2,3,32]{2,0,1:T(2,128)S(1)}, u32[]{:S(2)}, u32[]{:S(2)}) collective-permute-start(f32[2,3,32]{2,0,1:T(2,128)S(1)} %collective-permute-done.6), channel_id=1, source_target_pairs={{0,1},{1,2},{2,3},{3,4},{4,5},{5,6},{6,7},{7,8},{8,9},{9,10},{10,1... | collective-permute-start | bytes 2312 | tf_op jit(solution)/shard_map/ppermute | solution.py:145
  99.4 5.7 %collective-permute-start.8 = (f32[2,3,32]{2,0,1:T(2,128)S(1)}, f32[2,3,32]{2,0,1:T(2,128)S(1)}, u32[]{:S(2)}, u32[]{:S(2)}) collective-permute-start(f32[2,3,32]{2,0,1:T(2,128)S(1)} %collective-permute-done.7), channel_id=1, source_target_pairs={{0,1},{1,2},{2,3},{3,4},{4,5},{5,6},{6,7},{7,8},{8,9},{9,10},{10,1... | collective-permute-start | bytes 2312 | tf_op jit(solution)/shard_map/ppermute | solution.py:145
  105.2 5.7 %collective-permute-start.9 = (f32[2,3,32]{2,0,1:T(2,128)S(1)}, f32[2,3,32]{2,0,1:T(2,128)S(1)}, u32[]{:S(2)}, u32[]{:S(2)}) collective-permute-start(f32[2,3,32]{2,0,1:T(2,128)S(1)} %collective-permute-done.8), channel_id=1, source_target_pairs={{0,1},{1,2},{2,3},{3,4},{4,5},{5,6},{6,7},{7,8},{8,9},{9,10},{10,1... | collective-permute-start | bytes 2312 | tf_op jit(solution)/shard_map/ppermute | solution.py:145
  111.0 5.7 %collective-permute-start.10 = (f32[2,3,32]{2,0,1:T(2,128)S(1)}, f32[2,3,32]{2,0,1:T(2,128)S(1)}, u32[]{:S(2)}, u32[]{:S(2)}) collective-permute-start(f32[2,3,32]{2,0,1:T(2,128)S(1)} %collective-permute-done.9), channel_id=1, source_target_pairs={{0,1},{1,2},{2,3},{3,4},{4,5},{5,6},{6,7},{7,8},{8,9},{9,10},{10,1... | collective-permute-start | bytes 2312 | tf_op jit(solution)/shard_map/ppermute | solution.py:145
  116.8 5.7 %collective-permute-start.11 = (f32[2,3,32]{2,0,1:T(2,128)S(1)}, f32[2,3,32]{2,0,1:T(2,128)S(1)}, u32[]{:S(2)}, u32[]{:S(2)}) collective-permute-start(f32[2,3,32]{2,0,1:T(2,128)S(1)} %collective-permute-done.10), channel_id=1, source_target_pairs={{0,1},{1,2},{2,3},{3,4},{4,5},{5,6},{6,7},{7,8},{8,9},{9,10},{10,1... | collective-permute-start | bytes 2312 | tf_op jit(solution)/shard_map/ppermute | solution.py:145
  122.7 5.7 %collective-permute-start.12 = (f32[2,3,32]{2,0,1:T(2,128)S(1)}, f32[2,3,32]{2,0,1:T(2,128)S(1)}, u32[]{:S(2)}, u32[]{:S(2)}) collective-permute-start(f32[2,3,32]{2,0,1:T(2,128)S(1)} %collective-permute-done.11), channel_id=1, source_target_pairs={{0,1},{1,2},{2,3},{3,4},{4,5},{5,6},{6,7},{7,8},{8,9},{9,10},{10,1... | collective-permute-start | bytes 2312 | tf_op jit(solution)/shard_map/ppermute | solution.py:145
  128.5 5.7 %collective-permute-start.13 = (f32[2,3,32]{2,0,1:T(2,128)S(1)}, f32[2,3,32]{2,0,1:T(2,128)S(1)}, u32[]{:S(2)}, u32[]{:S(2)}) collective-permute-start(f32[2,3,32]{2,0,1:T(2,128)S(1)} %collective-permute-done.12), channel_id=1, source_target_pairs={{0,1},{1,2},{2,3},{3,4},{4,5},{5,6},{6,7},{7,8},{8,9},{9,10},{10,1... | collective-permute-start | bytes 2312 | tf_op jit(solution)/shard_map/ppermute | solution.py:145
  134.3 5.7 %collective-permute-start.14 = (f32[2,3,32]{2,0,1:T(2,128)S(1)}, f32[2,3,32]{2,0,1:T(2,128)S(1)}, u32[]{:S(2)}, u32[]{:S(2)}) collective-permute-start(f32[2,3,32]{2,0,1:T(2,128)S(1)} %collective-permute-done.13), channel_id=1, source_target_pairs={{0,1},{1,2},{2,3},{3,4},{4,5},{5,6},{6,7},{7,8},{8,9},{9,10},{10,1... | collective-permute-start | bytes 2312 | tf_op jit(solution)/shard_map/ppermute | solution.py:145
  151.6 3.5 %copy-start.3 = (f32[3,8192]{0,1:T(8,128)S(1)}, f32[3,8192]{0,1:T(8,128)}, u32[]{:S(2)}) copy-start(f32[3,8192]{0,1:T(8,128)} %scatter_custom_fusion) | copy-start | bytes 294916
  151.6 3.5 %copy-start.16 = (f32[19,3,1]{0,1,2:T(4,128)S(1)}, f32[19,3,1]{0,1,2:T(4,128)}, u32[]{:S(2)}) copy-start(f32[19,3,1]{0,1,2:T(4,128)} %constant.200) | copy-start | bytes 688
  155.1 7.1 %copy-start.2 = (f32[3,8192]{0,1:T(8,128)S(1)}, f32[3,8192]{0,1:T(8,128)}, u32[]{:S(2)}) copy-start(f32[3,8192]{0,1:T(8,128)} %scatter_custom_fusion.1) | copy-start | bytes 294916
  160.1 9.1 %collective-permute-start.15 = (f32[19,1,64,128]{3,2,1,0:T(8,128)S(1)}, f32[19,1,64,128]{3,2,1,0:T(8,128)S(1)}, u32[]{:S(2)}, u32[]{:S(2)}) collective-permute-start(f32[19,1,64,128]{3,2,1,0:T(8,128)S(1)} %get-tuple-element.80), channel_id=1, source_target_pairs={{0,1},{1,2},{2,3},{3,4},{4,5},{5,6},{6,7},{7,8},{8,9},{9,10},{10,1... | collective-permute-start | bytes 1867784 | tf_op jit(solution)/shard_map/ppermute | solution.py:44
  162.2 6.9 %copy-start.18 = (f32[19]{0:T(128)S(1)}, f32[19]{0:T(128)}, u32[]{:S(2)}) copy-start(f32[19]{0:T(128)} %constant.191.clone) | copy-start | bytes 232
  170.9 0.7 copy-start.11
  171.6 1.7 copy-start.15
  175.1 0.7 copy-start.13
  178.1 4.6 %copy-start.10 = (pred[2,64,128]{2,1,0:T(8,128)(4,1)S(1)}, pred[2,64,128]{2,1,0:T(8,128)(4,1)}, u32[]{:S(2)}) copy-start(pred[2,64,128]{2,1,0:T(8,128)(4,1)} %get-tuple-element.37) | copy-start | bytes 49156
  178.1 4.8 %copy-start.9 = (pred[2,64,128]{2,1,0:T(8,128)(4,1)S(1)}, pred[2,64,128]{2,1,0:T(8,128)(4,1)}, u32[]{:S(2)}) copy-start(pred[2,64,128]{2,1,0:T(8,128)(4,1)} %get-tuple-element.35) | copy-start | bytes 49156
  178.2 4.8 %copy-start.8 = (pred[2,64,128]{2,1,0:T(8,128)(4,1)S(1)}, pred[2,64,128]{2,1,0:T(8,128)(4,1)}, u32[]{:S(2)}) copy-start(pred[2,64,128]{2,1,0:T(8,128)(4,1)} %get-tuple-element.33) | copy-start | bytes 49156
  178.2 6.8 %copy-start.7 = (pred[2,64,128]{2,1,0:T(8,128)(4,1)S(1)}, pred[2,64,128]{2,1,0:T(8,128)(4,1)}, u32[]{:S(2)}) copy-start(pred[2,64,128]{2,1,0:T(8,128)(4,1)} %get-tuple-element.31) | copy-start | bytes 49156
  178.3 15.3 %collective-permute-start.17 = (f32[19,1,64,128]{3,2,0,1:T(8,128)S(1)}, f32[19,1,64,128]{3,2,0,1:T(8,128)S(1)}, u32[]{:S(2)}, u32[]{:S(2)}) collective-permute-start(f32[19,1,64,128]{3,2,0,1:T(8,128)S(1)} %get-tuple-element.67), channel_id=1, source_target_pairs={{0,1},{1,2},{2,3},{3,4},{4,5},{5,6},{6,7},{7,8},{8,9},{9,10},{10,1... | collective-permute-start | bytes 1867784 | tf_op jit(solution)/shard_map/ppermute | solution.py:44
  183.1 11.6 %collective-permute-start.18 = (f32[19,1,64,128]{3,2,0,1:T(8,128)S(1)}, f32[19,1,64,128]{3,2,0,1:T(8,128)S(1)}, u32[]{:S(2)}, u32[]{:S(2)}) collective-permute-start(f32[19,1,64,128]{3,2,0,1:T(8,128)S(1)} %get-tuple-element.66), channel_id=1, source_target_pairs={{1,0},{2,1},{3,2},{4,3},{5,4},{6,5},{7,6},{8,7},{9,8},{10,9},{11,1... | collective-permute-start | bytes 1867784 | tf_op jit(solution)/shard_map/ppermute | solution.py:45
  196.5 1.0 copy-start.19
